TPU v7x, 512 devices: a whole 4x8x8 slice. The times are simulated.
512 devices in a mesh: pair: 2 (over y_hi), blk: 32 (over y_lo, z), group: 8 (over x, core).
Axes of the slice: x: 4, y: 8 (y_hi: 2, y_lo: 4; y = y_hi * 4 + y_lo), z: 8, core: 2. Of those that a mesh axis runs over, the one named last changes fastest.
Arguments:
- codes: int32 [512, 1536, 256], P(('pair', 'blk', 'group')), may hold values from 0 to 255
- scales: int32 [512, 1536, 8], P(('pair', 'blk', 'group')), may hold values from -7 to 0
- inputs: bfloat16 [65536, 1536], P(('pair', 'blk', 'group')), may hold values from -6 to 6
- cotangent: bfloat16 [65536, 256], P(('pair', 'blk', 'group')), may hold values from -6 to 6
Outputs:
- earlier_grad: float32 [1536, 256], replicated
- current_grad: float32 [1536, 256], replicated
All inputs are finite; a program needn't handle non-finite values.
Results may differ from a plain program's by a relative error of at most 0.0003.
Values sent between devices are 32-bit elements; how exact they have to be, the bound alone decides.
A program may use at most 64 MiB of HBM per device.

v0:
```python
import jax
import jax.numpy as jnp
from jax import lax
from jax.sharding import Mesh
from jax.sharding import PartitionSpec as P

PAIR_BLK = ("pair", "blk_0", "blk_1")
BLK = ("blk_0", "blk_1")
PAIR_BLK_GROUP = ("pair", "blk_0", "blk_1", "group")


def reduced_to_own(blocks, axes, turns):
    dims = [lax.axis_size(a) for a in axes]
    blocks = blocks.reshape(*dims, *blocks.shape[1:])
    blocks = blocks.transpose(*turns, *range(len(axes), blocks.ndim))
    blocks = blocks.reshape(-1, *blocks.shape[len(axes) :])
    for k in turns:
        blocks = lax.psum_scatter(blocks, axes[k], scatter_dimension=0, tiled=True)
    return blocks[0]


def cut_along(x, dim, peers):
    dims = x.shape
    blocks = x.reshape(*dims[:dim], peers, dims[dim] // peers, *dims[dim + 1 :])
    return jnp.moveaxis(blocks, dim, 0)


def summed_rows(x, axes, turns, dim):
    peers = lax.axis_size(axes)
    return reduced_to_own(cut_along(x, dim, peers), axes, turns)


def from_everyone(x, axis):
    peers = lax.axis_size(axis)
    return lax.all_to_all(jnp.broadcast_to(x[None], (peers, *x.shape)), axis, 0, 0, tiled=True)


def of_everyone(x, axis):
    everything = from_everyone(x, axis)
    return jnp.sum(everything, axis=0)


def decode(codes, scales):
    codes = codes[0]
    scales = scales[0]
    rows, width = codes.shape
    sign = 1.0 - 2.0 * (codes // 128).astype(jnp.float32)
    field = codes // 8 % 16
    mant = (codes % 8).astype(jnp.float32)
    frac = jnp.where(field > 0, 8.0 + mant, mant)
    power = jnp.where(field > 0, field, 1) - 10
    expo = power.reshape(rows, scales.shape[1], width // scales.shape[1]) + scales[:, :, None]
    return sign * frac * jnp.exp2(expo.reshape(rows, width).astype(jnp.float32))


def combine(stack, count):
    share = summed_rows(stack, PAIR_BLK, (2, 1, 0), 1)
    total = of_everyone(share, "group") / count
    return lax.all_gather(total, PAIR_BLK, axis=1, tiled=True)


def key_product(inputs, cotangent):
    return lax.dot_general(
        inputs, cotangent, (((0,), (0,)), ((), ())), preferred_element_type=jnp.float32
    )


def local(codes, scales, inputs, cotangent):
    count = lax.axis_size("pair") * lax.axis_size(BLK) * lax.axis_size("group")
    decoded = decode(codes, scales)
    product = key_product(inputs, cotangent)
    summed = combine(jnp.stack([decoded, product]), count)
    earlier_grad = summed[0]
    current_grad = summed[1]
    return (earlier_grad, current_grad)


def solution(mesh):
    split = Mesh(
        mesh.devices.reshape(mesh.shape["pair"], 4, 8, mesh.shape["group"]),
        ("pair", "blk_0", "blk_1", "group"),
    )
    in_specs = (
        P(PAIR_BLK_GROUP, None, None),
        P(PAIR_BLK_GROUP, None, None),
        P(PAIR_BLK_GROUP, None),
        P(PAIR_BLK_GROUP, None),
    )
    out_specs = (P(), P())
    return jax.shard_map(local, mesh=split, in_specs=in_specs, out_specs=out_specs, check_vma=False)
```

profile of v0, /device:TPU:1, one launch (start us, length us, event | category | flops | bytes accessed | tf_op | source)
XLA Modules:
  0.0 228.9 jit_solution(12338459696429751346)
XLA Ops:
  7.2 0.0 copy-start
  7.2 0.0 reduce-scatter.4.cloned.1.call-start
  7.2 1.9 copy.19
  9.1 4.1 %fusion.5 = f32[1,1536,256]{1,2,0:T(8,128)S(1)} fusion(s32[1,1536,256]{1,2,0:T(8,128)S(1)} %copy.19, s32[1536,8]{0,1:T(8,128)} %bitcast.23), kind=kLoop, calls=%fused_computation.19 | loop fusion | flops 21233664 | bytes 3194880 | tf_op jit(solution)/shard_map/mul | solution.py:53
  13.2 0.5 copy.23
  13.7 0.0 copy-done
  13.7 1.2 fusion.15
  15.0 0.2 pad_maximum_fusion
  15.2 2.1 copy.25
  17.3 0.0 reduce-scatter.4.cloned.1.call-update
  17.3 0.0 reduce-scatter.6.cloned.1.call-start
  17.4 52.9 %reduce-scatter.4.cloned.1.call-done = f32[8,2,24,256]{3,2,1,0:T(8,128)} async-done(((f32[64,2,24,256]{3,2,1,0:T(8,128)}), f32[8,2,24,256]{3,2,1,0:T(8,128)}) %reduce-scatter.4.cloned.1.call-update) | async-done | bytes 393232 | tf_op jit(solution)/shard_map/reduce_scatter | solution.py:18
  70.3 0.0 reduce-scatter.6.cloned.1.call-update
  70.3 0.0 reduce-scatter.8.cloned.1.call-start
  70.4 31.2 %reduce-scatter.6.cloned.1.call-done = f32[2,2,24,256]{3,2,1,0:T(8,128)} async-done(((f32[8,2,24,256]{3,2,1,0:T(8,128)}), f32[2,2,24,256]{3,2,1,0:T(8,128)}) %reduce-scatter.6.cloned.1.call-update) | async-done | bytes 98320 | tf_op jit(solution)/shard_map/reduce_scatter | solution.py:18
  101.5 0.0 reduce-scatter.8.cloned.1.call-update
  101.5 0.0 all-gather.2.cloned.1.call-start
  101.6 26.3 %reduce-scatter.8.cloned.1.call-done = f32[1,2,24,256]{3,2,1,0:T(8,128)} async-done(((f32[2,2,24,256]{3,2,1,0:T(8,128)}), f32[1,2,24,256]{3,2,1,0:T(8,128)}) %reduce-scatter.8.cloned.1.call-update) | async-done | bytes 49168 | tf_op jit(solution)/shard_map/reduce_scatter | solution.py:18
  127.9 0.8 broadcast_in_dim.10
  128.7 12.0 %all_to_all.5 = f32[8,2,24,256]{3,2,1,0:T(8,128)S(1)} all-to-all(f32[8,2,24,256]{3,2,1,0:T(8,128)S(1)} %broadcast_in_dim.10), channel_id=1, replica_groups=mesh['pair'=2,'blk_0'=4,'blk_1'=8,'group'=8] {'group'}, dimensions={0} | all-to-all | bytes 786432 | tf_op jit(solution)/shard_map/all_to_all | solution.py:35
  140.7 0.6 broadcast_multiply_fusion
  141.4 0.0 all-gather.2.cloned.1.call-update
  141.4 77.2 %all-gather.2.cloned.1.call-done = f32[2,1536,256]{2,1,0:T(8,128)} async-done(((f32[2,24,256]{2,1,0:T(8,128)}), f32[2,1536,256]{2,1,0:T(8,128)}) %all-gather.2.cloned.1.call-update) | async-done | bytes 3145744 | tf_op jit(solution)/shard_map/all_gather | solution.py:59
  218.6 3.7 %slice_bitcast_fusion = (f32[1536,256]{1,0:T(8,128)}, f32[1536,256]{1,0:T(8,128)}) fusion(f32[2,1536,256]{2,1,0:T(8,128)} %all-gather.2.cloned.1.call-done), kind=kLoop, calls=%fused_computation.27 | loop fusion | bytes 6291456 | tf_op jit(solution)/shard_map/squeeze | solution.py:74
  (1 shorter events, 0.0 us)
Async XLA Ops:
  7.2 6.6 %copy-start = (bf16[128,1536]{1,0:T(8,128)(2,1)S(1)}, bf16[128,1536]{1,0:T(8,128)(2,1)}, u32[]{:S(2)}) copy-start(bf16[128,1536]{1,0:T(8,128)(2,1)} %param.6) | copy-start | bytes 1179652
  7.2 63.1 %reduce-scatter.4.cloned.1.call-start = ((), (), s32[]{:S(2)}) async-start(), calls=%async_computation.4 | async-start | bytes 3538944 | tf_op jit(solution)/shard_map/reduce_scatter | solution.py:18
  17.3 84.2 %reduce-scatter.6.cloned.1.call-start = ((), (), s32[]{:S(2)}) async-start(), calls=%async_computation.5 | async-start | bytes 491520 | tf_op jit(solution)/shard_map/reduce_scatter | solution.py:18
  70.3 57.5 %reduce-scatter.8.cloned.1.call-start = ((), (), s32[]{:S(2)}) async-start(), calls=%async_computation.6 | async-start | bytes 147456 | tf_op jit(solution)/shard_map/reduce_scatter | solution.py:18
  101.5 117.1 %all-gather.2.cloned.1.call-start = ((), (), s32[]{:S(2)}) async-start(), calls=%async_computation.7 | async-start | bytes 3194880 | tf_op jit(solution)/shard_map/all_gather | solution.py:59
Sparse Core Ops, SparseCore 0:
  17.5 52.7 reduce-scatter.3
  73.1 28.3 reduce-scatter.5
  104.3 23.5 reduce-scatter.7
  141.5 77.0 all-gather.1
where the time goes:
time: 232 us; the launch traced here: 229 us
  waiting for transfers between devices  188 us (81%)
  between operations  13.8 us (6%)
  blocking collectives  12 us (5%)
  local copies, waits for them, and re-layouts  9.08 us (4%)
  other arithmetic  4.95 us (2%)
    reduce_scatter x3, waiting for transfers between devices, reduced_to_own(): blocks = lax.psum_scatter(blocks, axes[k], scatter_dimension=0, tiled=True)  110 us
    all_gather x1, waiting for transfers between devices, combine(): return lax.all_gather(total, PAIR_BLK, axis=1, tiled=True)  77.2 us
    all_to_all x1, blocking collectives, from_everyone(): lax.all_to_all(jnp.broadcast_to(x[None], (peers, *x.shape)), axis, 0, 0,...  12 us
  transfers between devices with their start and end apart: 4, of which 4 were waited for; matrix products, arithmetic and copies ran while one was open for 0% of the time, Pallas kernels for 0%

commit v1 on v0

v1 whole, which is shorter than its diff:
```python
import functools

import jax
import jax.numpy as jnp
from jax import lax
from jax.experimental import pallas as pl
from jax.experimental.pallas import tpu as pltpu
from jax.sharding import PartitionSpec as P

EVERY = ("pair", "blk", "group")
MESH_ID = pl.DeviceIdType.MESH
NX, NY, NZ = 4, 8, 8
RING = 8
HALF = RING // 2
BLOCK = 3
PAIR = 2 * BLOCK
CHUNK = RING * BLOCK
OWN = RING * CHUNK
ALL = 2 * OWN
SUBS = 4
OFFSETS = (2, 1, 3, 0)
TILE = (8, 128)


def steps_of(direction, sub):
    return HALF if (sub < SUBS // 2) == (direction == 0) else HALF - 1


def rem(a, n):
    return lax.rem(a, jnp.int32(n))


def div(a, n):
    return lax.div(a, jnp.int32(n))


def kernel(
    codes_ref, scales_ref, inputs_ref, cot_ref, out0, out1,
    codes_v, scales_v, inputs_v, cot_v,
    part0, part1, peer0, peer1, ring_in, ring_out, chunk_sum, block_in, x_in,
    load_sem, peer_sem, ring_sem, block_sem, x_sem, owner_sem, spread_sem, final_sem, send_sem,
):
    outs, parts, peers = (out0, out1), (part0, part1), (peer0, peer1)
    group = lax.axis_index("group")
    blk = lax.axis_index("blk")
    x, core = div(group, 2), rem(group, 2)
    y, z = lax.axis_index("pair") * 4 + div(blk, 8), rem(blk, 8)

    def device(x, y, z, core):
        return (div(y, 4), rem(y, 4) * 8 + z, x * 2 + core)

    def along_first(color, to):
        return device(x, to, z, core) if color == 0 else device(x, y, to, core)

    def along_second(color, to):
        return device(x, y, to, core) if color == 0 else device(x, to, z, core)

    first = (y, z)
    second = (z, y)
    partner = device(x, y, z, 1 - core)

    loads = [
        pltpu.make_async_copy(src, dst, load_sem.at[i])
        for i, (src, dst) in enumerate(
            ((codes_ref, codes_v), (scales_ref, scales_v), (inputs_ref, inputs_v), (cot_ref, cot_v))
        )
    ]
    for load in loads:
        load.start()

    barrier = pltpu.get_barrier_semaphore()
    greeted = [partner]
    greeted += [device(rem(x + d, NX), y, z, core) for d in range(1, NX)]
    greeted += [device(x, rem(y + d, NY), z, core) for d in range(1, NY)]
    greeted += [device(x, y, rem(z + d, NZ), core) for d in range(1, NZ)]
    for other in greeted:
        pl.semaphore_signal(barrier, inc=1, device_id=other, device_id_type=MESH_ID)

    for load in loads:
        load.wait()

    lane_block = lax.broadcasted_iota(jnp.int32, (8, 256), 1) // 32
    spread = (lane_block == lax.broadcasted_iota(jnp.int32, (8, 256), 0)).astype(jnp.float32)

    def compute(i, carry):
        rows = pl.ds(pl.multiple_of(i * 128, 128), 128)
        code = codes_v[rows, :]
        field = (code >> 3) & 15
        mant = code & 7
        magnitude = jnp.where(field > 0, mant + 8, mant) << jnp.maximum(field - 1, 0)
        signed = jnp.where(code >= 128, -magnitude, magnitude).astype(jnp.float32)
        powers = jnp.exp2((scales_v[:, rows] - 9).astype(jnp.float32))
        scale = lax.dot_general(
            powers, spread, (((0,), (0,)), ((), ())), preferred_element_type=jnp.float32
        )
        decoded = signed * scale
        product = lax.dot_general(
            inputs_v[:, rows], cot_v[...], (((0,), (0,)), ((), ())),
            preferred_element_type=jnp.float32,
        )
        for part, value in ((part0, decoded), (part1, product)):
            for r in range(16):
                for t in range(2):
                    part[32 * i + 2 * r + t] = value[8 * r : 8 * r + 8, 128 * t : 128 * t + 128]
        return carry

    lax.fori_loop(0, 12, compute, 0)

    pl.semaphore_wait(barrier, len(greeted))

    def send(src, dst, sent, received, to):
        pltpu.make_async_remote_copy(
            src_ref=src, dst_ref=dst, send_sem=sent, recv_sem=received,
            device_id=to, device_id_type=MESH_ID,
        ).start()

    def wait_for(ref, sem):
        pltpu.make_async_copy(ref, ref, sem).wait()

    reach = [HALF] + [s * d for d in range(HALF - 1, 0, -1) for s in (1, -1)] + [0]
    for d in reach:
        for color in range(2):
            at = rem(first[color] + d + RING, RING) * CHUNK
            send(
                parts[color].at[pl.ds((1 - core) * OWN + at, CHUNK)],
                peers[color].at[pl.ds(at, CHUNK)],
                send_sem.at[color, 0],
                peer_sem.at[color, d + HALF - 1],
                partner,
            )

    pairs = [[rem(div(second[q], 2) + o, SUBS) for o in OFFSETS] for q in range(2)]

    def chip_sum(color, chunk, sub):
        at = chunk * CHUNK + pairs[color][sub] * PAIR
        return parts[color][pl.ds(core * OWN + at, PAIR)] + peers[color][pl.ds(at, PAIR)]

    for step in range(HALF):
        left = HALF - step
        for d in ((HALF,) if left == HALF else (left, -left)):
            for color in range(2):
                wait_for(peers[color].at[pl.ds(0, CHUNK)], peer_sem.at[color, d + HALF - 1])
        for sub in range(SUBS):
            for color in range(2):
                for direction, sign in ((0, 1), (1, -1)):
                    if steps_of(direction, sub) < left:
                        continue
                    value = chip_sum(color, rem(first[color] + sign * left + RING, RING), sub)
                    if steps_of(direction, sub) > left:
                        arrived = ring_in.at[color, direction, step - 1, sub]
                        wait_for(arrived, ring_sem.at[color, direction, step - 1, sub])
                        value = value + arrived[...]
                    ring_out[color, direction, step, sub] = value
                    send(
                        ring_out.at[color, direction, step, sub],
                        ring_in.at[color, direction, step, sub],
                        send_sem.at[color, 1],
                        ring_sem.at[color, direction, step, sub],
                        along_first(color, rem(first[color] + sign + RING, RING)),
                    )

    for color in range(2):
        wait_for(peers[color].at[pl.ds(0, CHUNK)], peer_sem.at[color, HALF - 1])
    for sub in range(SUBS):
        for color in range(2):
            value = chip_sum(color, first[color], sub)
            for direction in range(2):
                arrived = ring_in.at[color, direction, HALF - 1, sub]
                wait_for(arrived, ring_sem.at[color, direction, HALF - 1, sub])
                value = value + arrived[...]
            chunk_sum[color, pl.ds(pairs[color][sub] * PAIR, PAIR)] = value
            if OFFSETS[sub]:
                owners = [pairs[color][sub] * 2, pairs[color][sub] * 2 + 1]
            else:
                owners = [second[color] + 1 - 2 * rem(second[color], 2)]
            for owner in owners:
                send(
                    chunk_sum.at[color, pl.ds(owner * BLOCK, BLOCK)],
                    block_in.at[color, rem(second[color] - owner + RING, RING) - 1],
                    send_sem.at[color, 2],
                    block_sem.at[color],
                    along_second(color, owner),
                )

    for color in range(2):
        wait_for(block_in.at[color], block_sem.at[color])
        value = chunk_sum[color, pl.ds(second[color] * BLOCK, BLOCK)]
        for slot in range(RING - 1):
            value = value + block_in[color, slot]
        x_in[color, x] = value
        for d in (2, 1, 3):
            send(
                x_in.at[color, x],
                x_in.at[color, x],
                send_sem.at[color, 3],
                x_sem.at[color],
                device(rem(x + d, NX), y, z, core),
            )

    def place(color, chunk):
        return core * OWN + chunk * CHUNK

    count = 2.0 * NX * NY * NZ
    for color in range(2):
        wait_for(x_in.at[color, pl.ds(0, NX - 1)], x_sem.at[color])
        total = x_in[color, 0]
        for k in range(1, NX):
            total = total + x_in[color, k]
        mine = pl.ds(place(color, first[color]) + second[color] * BLOCK, BLOCK)
        outs[color][mine] = total * (1.0 / count)
        for d in (4, 3, 5, 2, 6, 1, 7):
            other = rem(second[color] + d, RING)
            offset = rem(div(second[color], 2) - div(other, 2) + SUBS, SUBS)
            send(
                outs[color].at[mine],
                outs[color].at[mine],
                send_sem.at[color, 4],
                owner_sem.at[color, offset],
                along_second(color, other),
            )

    events = []
    for sub in range(SUBS):
        ready = {0: 1.9, 1: 3.1, 3: 3.1, 2: 4.0}[OFFSETS[sub]]
        for step in range(HALF + 1):
            events.append((ready + 1.9 * step, step, sub))
    for _, step, sub in sorted(events):
        for color in range(2):
            for direction, sign in ((0, 1), (1, -1)):
                if step > steps_of(direction, sub) or (step == 0 and direction == 1):
                    continue
                chunk = rem(first[color] - sign * step + RING, RING)
                here = outs[color].at[
                    pl.ds(place(color, chunk) + pairs[color][sub] * PAIR, PAIR)
                ]
                if step == 0:
                    size = PAIR if OFFSETS[sub] else BLOCK
                    wait_for(
                        outs[color].at[pl.ds(0, size)], owner_sem.at[color, OFFSETS[sub]]
                    )
                else:
                    wait_for(here, spread_sem.at[color, direction, step - 1, sub])
                for way, turn in ((0, 1), (1, -1)):
                    if (step == 0 or way == direction) and step < steps_of(way, sub):
                        send(
                            here,
                            here,
                            send_sem.at[color, 5],
                            spread_sem.at[color, way, step, sub],
                            along_first(color, rem(first[color] + turn + RING, RING)),
                        )
                send(here, here, send_sem.at[color, 6], final_sem.at[color], partner)

    sent = (OWN, 28 * PAIR, 7 * BLOCK, 3 * BLOCK, 7 * BLOCK, 28 * PAIR, OWN)
    for color in range(2):
        wait_for(outs[color].at[pl.ds(0, OWN)], final_sem.at[color])
        for kind, tiles in enumerate(sent):
            wait_for(parts[color].at[pl.ds(0, tiles)], send_sem.at[color, kind])


def summed(codes, scales, inputs, cotangent):
    tiles = jax.ShapeDtypeStruct((ALL, *TILE), jnp.float32)
    dma = pltpu.SemaphoreType.DMA
    return pl.pallas_call(
        kernel,
        name="sum_everywhere",
        out_shape=(tiles, tiles),
        in_specs=[pl.BlockSpec(memory_space=pltpu.HBM)] * 4,
        out_specs=[pl.BlockSpec(memory_space=pltpu.VMEM)] * 2,
        scratch_shapes=[
            pltpu.VMEM(codes.shape, jnp.int32),
            pltpu.VMEM(scales.shape, jnp.int32),
            pltpu.VMEM(inputs.shape, inputs.dtype),
            pltpu.VMEM(cotangent.shape, cotangent.dtype),
            pltpu.VMEM((ALL, *TILE), jnp.float32),
            pltpu.VMEM((ALL, *TILE), jnp.float32),
            pltpu.VMEM((OWN, *TILE), jnp.float32),
            pltpu.VMEM((OWN, *TILE), jnp.float32),
            pltpu.VMEM((2, 2, HALF, SUBS, PAIR, *TILE), jnp.float32),
            pltpu.VMEM((2, 2, HALF, SUBS, PAIR, *TILE), jnp.float32),
            pltpu.VMEM((2, CHUNK, *TILE), jnp.float32),
            pltpu.VMEM((2, RING - 1, BLOCK, *TILE), jnp.float32),
            pltpu.VMEM((2, NX, BLOCK, *TILE), jnp.float32),
            dma((4,)),
            dma((2, 2 * HALF)),
            dma((2, 2, HALF, SUBS)),
            dma((2,)),
            dma((2,)),
            dma((2, SUBS)),
            dma((2, 2, HALF, SUBS)),
            dma((2,)),
            dma((2, 7)),
        ],
        compiler_params=pltpu.CompilerParams(
            collective_id=0, has_side_effects=True, vmem_limit_bytes=40 << 20
        ),
    )(codes, scales, inputs, cotangent)


def untiled(tiles, shape):
    rows, columns = shape
    grid = tiles.reshape(rows // 8, columns // 128, *TILE)
    return grid.transpose(0, 2, 1, 3).reshape(shape)


def local(codes, scales, inputs, cotangent):
    shape = codes.shape[1:]
    earlier, current = summed(codes[0], scales[0].T, inputs, cotangent)
    return untiled(earlier, shape), untiled(current, shape)


def solution(mesh):
    in_specs = (
        P(EVERY, None, None),
        P(EVERY, None, None),
        P(EVERY, None),
        P(EVERY, None),
    )
    return jax.shard_map(
        local, mesh=mesh, in_specs=in_specs, out_specs=(P(), P()), check_vma=False
    )
```

time: 232 us -> 70.5 us (0.30); the launches traced: 229 us -> 70.2 us
  waiting for transfers between devices: 188 us -> 0 us
  Pallas kernels: 0 us -> 63.3 us
  between operations: 13.8 us -> 0.65 us
  blocking collectives: 12 us -> 0 us
  other arithmetic: 4.95 us -> 0 us
  local copies, waits for them, and re-layouts: 9.08 us -> 6.32 us
    reduce_scatter x3 -> x0, waiting for transfers between devices: 110 us -> none  [reduced_to_own(): blocks = lax.psum_scatter(blocks, axes[k], scatter_dimension=0, tiled=True)]
    all_gather x1 -> x0, waiting for transfers between devices: 77.2 us -> none  [combine(): return lax.all_gather(total, PAIR_BLK, axis=1, tiled=True)]
    pallas_call x0 -> x1, Pallas kernels: none -> 63.3 us  [summed(): pl.pallas_call(kernel, name='sum_everywhere', out_shape=(tiles, tiles), i...]
    all_to_all x1 -> x0, blocking collectives: 12 us -> none  [from_everyone(): lax.all_to_all(jnp.broadcast_to(x[None], (peers, *x.shape)), axis, 0, 0,...]
    unnamed x3 -> x10, local copies, waits for them, and re-layouts: 1.92 us -> 6.32 us
    mul x1 -> x0, other arithmetic: 4.09 us -> none  [decode(): return sign * frac * jnp.exp2(expo.reshape(rows, width).astype(jnp.float32))]
    squeeze x1 -> x0, local copies, waits for them, and re-layouts: 3.74 us -> none  [local(): current_grad = summed[1]]
  transfers between devices with their start and end apart: 4 -> 0, of which waited for: 4 -> 0; matrix products, arithmetic and copies ran while one was open for 0% -> 0% of each run, Pallas kernels for 0% -> 0%
where the time goes in v1:
time: 70.5 us; the launch traced here: 70.2 us
  Pallas kernels  63.3 us (90%)
  local copies, waits for them, and re-layouts  6.32 us (9%)
    pallas_call x1, Pallas kernels, summed(): pl.pallas_call(kernel, name='sum_everywhere', out_shape=(tiles, tiles), i...  63.3 us
    unnamed x10, local copies, waits for them, and re-layouts  6.32 us

profile of v1, /device:TPU:1, one launch (start us, length us, event | category | flops | bytes accessed | tf_op | source)
XLA Modules:
  0.0 70.2 jit_solution(11145978071712280095)
XLA Ops:
  0.6 0.0 copy-start
  0.6 1.4 %copy-done = s32[1,1536,256]{2,1,0:T(8,128)S(1)} copy-done((s32[1,1536,256]{2,1,0:T(8,128)S(1)}, s32[1,1536,256]{2,1,0:T(8,128)}, u32[]{:S(2)}) %copy-start) | copy-done | bytes 1572888
  2.0 0.0 copy-start.1
  2.0 1.0 %copy-done.1 = bf16[128,1536]{1,0:T(8,128)(2,1)S(1)} copy-done((bf16[128,1536]{1,0:T(8,128)(2,1)S(1)}, bf16[128,1536]{1,0:T(8,128)(2,1)}, u32[]{:S(2)}) %copy-start.1) | copy-done | bytes 393240
  3.0 0.0 copy-start.2
  3.0 0.8 %copy-done.2 = bf16[128,256]{1,0:T(8,128)(2,1)S(1)} copy-done((bf16[128,256]{1,0:T(8,128)(2,1)S(1)}, bf16[128,256]{1,0:T(8,128)(2,1)}, u32[]{:S(2)}) %copy-start.2) | copy-done | bytes 65560
  3.9 0.0 copy-start.3
  3.9 0.8 %copy-done.3 = s32[1,1536,8]{1,2,0:T(8,128)S(1)} copy-done((s32[1,1536,8]{1,2,0:T(8,128)S(1)}, s32[1,1536,8]{1,2,0:T(8,128)}, u32[]{:S(2)}) %copy-start.3) | copy-done | bytes 49176
  4.7 63.3 %sum_everywhere.1 = (f32[384,8,128]{2,1,0:T(8,128)S(1)}, f32[384,8,128]{2,1,0:T(8,128)S(1)}) custom-call(s32[1536,256]{1,0:T(8,128)S(1)} %bitcast.16, s32[8,1536]{1,0:T(8,128)S(1)} %bitcast.17, bf16[128,1536]{1,0:T(8,128)(2,1)S(1)} %copy-done.1, bf16[128,256]{1,0:T(8,128)(2,1)S(1)} %copy-done.2), custom_call_target="tpu_custom_call" | custom-call | tf_op jit(solution)/shard_map/sum_everywhere/pallas_call | solution.py:264
  68.0 1.1 %copy.8 = f32[1536,256]{1,0:T(8,128)} copy(f32[1536,256]{1,0:T(8,128)S(1)} %bitcast.15) | data formatting | bytes 3145728
  69.1 1.1 %copy.9 = f32[1536,256]{1,0:T(8,128)} copy(f32[1536,256]{1,0:T(8,128)S(1)} %bitcast.14) | data formatting | bytes 3145728
Async XLA Ops:
  0.6 1.4 %copy-start = (s32[1,1536,256]{2,1,0:T(8,128)S(1)}, s32[1,1536,256]{2,1,0:T(8,128)}, u32[]{:S(2)}) copy-start(s32[1,1536,256]{2,1,0:T(8,128)} %param.4) | copy-start | bytes 4718596
  2.0 1.0 %copy-start.1 = (bf16[128,1536]{1,0:T(8,128)(2,1)S(1)}, bf16[128,1536]{1,0:T(8,128)(2,1)}, u32[]{:S(2)}) copy-start(bf16[128,1536]{1,0:T(8,128)(2,1)} %inputs_ref.1) | copy-start | bytes 1179652
  3.0 0.8 %copy-start.2 = (bf16[128,256]{1,0:T(8,128)(2,1)S(1)}, bf16[128,256]{1,0:T(8,128)(2,1)}, u32[]{:S(2)}) copy-start(bf16[128,256]{1,0:T(8,128)(2,1)} %cot_ref.1) | copy-start | bytes 196612
  3.9 0.8 %copy-start.3 = (s32[1,1536,8]{1,2,0:T(8,128)S(1)}, s32[1,1536,8]{1,2,0:T(8,128)}, u32[]{:S(2)}) copy-start(s32[1,1536,8]{1,2,0:T(8,128)} %param.5) | copy-start | bytes 147460
